TPU v7x, 32 devices: a whole 2x2x4 slice. The times are simulated.
32 devices in a mesh: dp: 2 (over y), head: 16 (over z, x, core).
Axes of the slice: x: 2, y: 2, z: 4, core: 2. Of those that a mesh axis runs over, the one named last changes fastest.
Arguments:
- head_ids: int32 [2, 2048, 8], P('dp', 'head'), may hold values from 0 to 63, as said below
- query_slots: bfloat16 [2, 2048, 8, 128], P('dp', 'head'), may hold values from -300 to 300
- key_slots: bfloat16 [2, 2048, 8, 128], P('dp', 'head'), may hold values from -13 to 13
- value_slots: bfloat16 [2, 2048, 8, 128], P('dp', 'head'), may hold values from -5 to 5
- gate_logits: float32 [2, 2048, 8], P('dp', 'head'), may hold values from -8 to 310
- sink_logits: float32 [64], P('head'), may hold values from 1 to 6
- out_grad: bfloat16 [2, 2048, 8, 128], P('dp', 'head'), may hold values from -6 to 6
Outputs:
- mixed: bfloat16 [2, 2048, 8, 128], P('dp', 'head')
- query_grad: bfloat16 [2, 2048, 8, 128], P('dp', 'head')
- key_grad: bfloat16 [2, 2048, 8, 128], P('dp', 'head')
- value_grad: bfloat16 [2, 2048, 8, 128], P('dp', 'head')
- gate_grad: float32 [2, 2048, 8], P('dp', 'head')
- sink_grad: float32 [64], P('head')
Inputs may be any that keep to these rules, and one draw needn't show every extreme that they name: `head_ids`: each token names 8 different heads. Among the 128 tokens of one device no head is named more than 32 times, and in every group one head is named exactly 32 times by the tokens of every device of that group.
All inputs are finite; a program needn't handle non-finite values.
Results may differ from a plain program's by a relative error of at most 0.023.
Values may be sent and summed in bfloat16 or wider, within the bound.
No kernel may reach another device: no remote copies, remote signals or barrier semaphores. Data moves between devices by JAX's collectives and lax.ppermute only.
A program may use at most 64 MiB of HBM per device.

v0:
```python
import math

import jax
import jax.numpy as jnp
from jax import lax
from jax.sharding import PartitionSpec as P

HEADS = 64
BLOCK = 512
SLOT = 32


masked_value = -1e30


def block_scores(query_tile, key_tile, query_live, key_live, query_offset, key_offset, scale):
    scores = scale * jnp.einsum(
        "qd,kd->qk", query_tile, key_tile, preferred_element_type=jnp.float32
    )
    query_index = query_offset + lax.iota(jnp.int32, query_tile.shape[0])
    key_index = key_offset + lax.iota(jnp.int32, key_tile.shape[0])
    allowed = query_live[:, None] & key_live[None, :] & (key_index[None, :] <= query_index[:, None])
    return (scores, allowed)


def forward_head(query_rows, key_rows, value_rows, live_rows, sink_value, used_blocks, width):
    row_count, head_width = query_rows.shape
    scale = 1.0 / math.sqrt(head_width)

    def forward_query_block(qblock, carry):
        lse_all, out_all = carry
        offset = qblock * width
        query_tile = lax.dynamic_slice_in_dim(query_rows, offset, width, 0)
        query_live = lax.dynamic_slice_in_dim(live_rows, offset, width, 0)

        def tile_at(kblock):
            key_offset = kblock * width
            key_tile = lax.dynamic_slice_in_dim(key_rows, key_offset, width, 0)
            value_tile = lax.dynamic_slice_in_dim(value_rows, key_offset, width, 0)
            key_live = lax.dynamic_slice_in_dim(live_rows, key_offset, width, 0)
            scores, allowed = block_scores(
                query_tile, key_tile, query_live, key_live, offset, key_offset, scale
            )
            return (scores, allowed, value_tile)

        def stat_step(kblock, state):
            run_max, run_sum = state
            scores, allowed, value_tile = tile_at(kblock)
            masked = jnp.where(allowed, scores, masked_value)
            new_max = jnp.maximum(run_max, jnp.max(masked, axis=1))
            new_sum = run_sum * jnp.exp(run_max - new_max) + jnp.sum(
                jnp.where(allowed, jnp.exp(masked - new_max[:, None]), 0.0), axis=1
            )
            return (new_max, new_sum)

        start_state = (jnp.full((width,), sink_value, jnp.float32), jnp.ones((width,), jnp.float32))
        run_max, run_sum = lax.fori_loop(0, qblock + 1, stat_step, start_state)
        row_lse = run_max + jnp.log(run_sum)

        def value_step(kblock, total):
            scores, allowed, value_tile = tile_at(kblock)
            weights = jnp.where(allowed, jnp.exp(scores - row_lse[:, None]), 0.0).astype(
                jnp.bfloat16
            )
            return total + jnp.dot(weights, value_tile, preferred_element_type=jnp.float32)

        total = lax.fori_loop(
            0, qblock + 1, value_step, jnp.zeros((width, head_width), jnp.float32)
        )
        lse_all = lax.dynamic_update_slice_in_dim(lse_all, row_lse, offset, 0)
        out_all = lax.dynamic_update_slice_in_dim(out_all, total.astype(jnp.bfloat16), offset, 0)
        return (lse_all, out_all)

    start_all = (
        jnp.zeros((row_count,), jnp.float32),
        jnp.zeros((row_count, head_width), jnp.bfloat16),
    )
    return lax.fori_loop(0, used_blocks, forward_query_block, start_all)


def backward_head(
    query_rows,
    key_rows,
    value_rows,
    cot_rows,
    head_out,
    lse_all,
    live_rows,
    sink_value,
    used_blocks,
    width,
):
    row_count, head_width = query_rows.shape
    scale = 1.0 / math.sqrt(head_width)
    deltas = jnp.sum(cot_rows.astype(jnp.float32) * head_out.astype(jnp.float32), axis=1)
    sink_term = -jnp.sum(jnp.exp(sink_value - lse_all) * deltas)

    def backward_query_block(qblock, carry):
        qgrad_all, kgrad_acc, vgrad_acc = carry
        offset = qblock * width
        query_tile = lax.dynamic_slice_in_dim(query_rows, offset, width, 0)
        cot_tile = lax.dynamic_slice_in_dim(cot_rows, offset, width, 0)
        lse_tile = lax.dynamic_slice_in_dim(lse_all, offset, width, 0)
        delta_tile = lax.dynamic_slice_in_dim(deltas, offset, width, 0)
        query_live = lax.dynamic_slice_in_dim(live_rows, offset, width, 0)

        def key_step(kblock, inner):
            qgrad_run, kgrad_acc, vgrad_acc = inner
            key_offset = kblock * width
            key_tile = lax.dynamic_slice_in_dim(key_rows, key_offset, width, 0)
            value_tile = lax.dynamic_slice_in_dim(value_rows, key_offset, width, 0)
            key_live = lax.dynamic_slice_in_dim(live_rows, key_offset, width, 0)
            scores, allowed = block_scores(
                query_tile, key_tile, query_live, key_live, offset, key_offset, scale
            )
            probability = jnp.where(allowed, jnp.exp(scores - lse_tile[:, None]), 0.0)
            weights = probability.astype(jnp.bfloat16)
            dprob = jnp.einsum(
                "qd,kd->qk", cot_tile, value_tile, preferred_element_type=jnp.float32
            )
            dscore = (probability * (dprob - delta_tile[:, None])).astype(jnp.bfloat16)
            qgrad_run = qgrad_run + jnp.dot(dscore, key_tile, preferred_element_type=jnp.float32)
            kgrad_part = jnp.einsum(
                "qk,qd->kd", dscore, query_tile, preferred_element_type=jnp.float32
            )
            vgrad_part = jnp.einsum(
                "qk,qd->kd", weights, cot_tile, preferred_element_type=jnp.float32
            )
            kgrad_acc = lax.dynamic_update_slice_in_dim(
                kgrad_acc,
                lax.dynamic_slice_in_dim(kgrad_acc, key_offset, width, 0) + kgrad_part,
                key_offset,
                0,
            )
            vgrad_acc = lax.dynamic_update_slice_in_dim(
                vgrad_acc,
                lax.dynamic_slice_in_dim(vgrad_acc, key_offset, width, 0) + vgrad_part,
                key_offset,
                0,
            )
            return (qgrad_run, kgrad_acc, vgrad_acc)

        start_inner = (jnp.zeros((width, head_width), jnp.float32), kgrad_acc, vgrad_acc)
        qgrad_run, kgrad_acc, vgrad_acc = lax.fori_loop(0, qblock + 1, key_step, start_inner)
        qgrad_all = lax.dynamic_update_slice_in_dim(
            qgrad_all, (scale * qgrad_run).astype(jnp.bfloat16), offset, 0
        )
        return (qgrad_all, kgrad_acc, vgrad_acc)

    start_all = (
        jnp.zeros((row_count, head_width), jnp.bfloat16),
        jnp.zeros((row_count, head_width), jnp.float32),
        jnp.zeros((row_count, head_width), jnp.float32),
    )
    qgrad_all, kgrad_acc, vgrad_acc = lax.fori_loop(0, used_blocks, backward_query_block, start_all)
    return (
        qgrad_all,
        (scale * kgrad_acc).astype(jnp.bfloat16),
        vgrad_acc.astype(jnp.bfloat16),
        sink_term,
    )


def arrange(live_rows, width):
    row_count = live_rows.shape[0]
    return (None, None, row_count // width)


def pick_rows(buffer, head_slot):
    picked = buffer[:, head_slot].reshape(-1, buffer.shape[-1])
    return picked


def restore(row_block, devices):
    return row_block.reshape(devices, -1, row_block.shape[-1])


def per_device(head_ids, query_slots, key_slots, value_slots, gate_logits, sink_logits, out_grad):
    devices = lax.axis_size("head")
    local_heads = HEADS // devices
    selected = head_ids[0]
    token_count, slot_count = selected.shape
    head_width = query_slots.shape[-1]
    matches = (selected[:, :, None] == lax.iota(jnp.int32, HEADS)[None, None, :]).astype(jnp.int32)
    per_token = jnp.sum(matches, axis=1)
    earlier = jnp.cumsum(per_token, axis=0) - per_token
    placing = jnp.sum(matches * earlier[:, None, :], axis=2)
    target = (selected * SLOT + placing).reshape(-1)
    buffer_rows = HEADS * SLOT

    def spread_out(flat_rows):
        filled_rows = (
            jnp.zeros((buffer_rows, flat_rows.shape[-1]), flat_rows.dtype).at[target].set(flat_rows)
        )
        return filled_rows.reshape(devices, local_heads, SLOT, flat_rows.shape[-1])

    def collect(buffer):
        return buffer.reshape(buffer_rows, buffer.shape[-1])[target].reshape(
            token_count, slot_count, buffer.shape[-1]
        )

    gate_probs = jax.nn.softmax(gate_logits[0], axis=-1)
    cotangent = (gate_probs[:, :, None] * out_grad[0].astype(jnp.float32)).astype(jnp.bfloat16)
    send_query = spread_out(query_slots[0].reshape(-1, head_width))
    send_key = spread_out(key_slots[0].reshape(-1, head_width))
    send_value = spread_out(value_slots[0].reshape(-1, head_width))
    send_cot = spread_out(cotangent.reshape(-1, head_width))
    filled = (
        jnp.zeros((buffer_rows,), jnp.bfloat16)
        .at[target]
        .set(jnp.ones((), jnp.bfloat16))
        .reshape(devices, local_heads, SLOT)
    )
    out_list, qgrad_list, kgrad_list, vgrad_list, sink_list = ([], [], [], [], [])
    recv_query, recv_key, recv_value, recv_fill = (
        lax.all_to_all(send_query, "head", split_axis=0, concat_axis=0, tiled=True),
        lax.all_to_all(send_key, "head", split_axis=0, concat_axis=0, tiled=True),
        lax.all_to_all(send_value, "head", split_axis=0, concat_axis=0, tiled=True),
        lax.all_to_all(filled, "head", split_axis=0, concat_axis=0, tiled=True),
    )
    prepared = []
    lse_list = []
    head_outs = []
    for head_slot in range(local_heads):
        live_rows = recv_fill[:, head_slot].reshape(-1) > 0
        gather_order, landing, used_blocks = arrange(live_rows, BLOCK)
        live_use = live_rows
        pieces = (
            pick_rows(recv_query, head_slot),
            pick_rows(recv_key, head_slot),
            pick_rows(recv_value, head_slot),
        )
        pieces, live_use, gather_order, landing, used_blocks = (
            pieces,
            live_use,
            gather_order,
            landing,
            used_blocks,
        )
        row_lse, head_out = forward_head(
            pieces[0], pieces[1], pieces[2], live_use, sink_logits[head_slot], used_blocks, BLOCK
        )
        prepared.append((pieces, live_use, gather_order, landing, used_blocks))
        lse_list.append(row_lse)
        head_outs.append(head_out)
        out_list.append(restore(head_out, devices))
    back_out = lax.all_to_all(
        jnp.stack(out_list, axis=1), "head", split_axis=0, concat_axis=0, tiled=True
    )
    recv_cot = lax.all_to_all(send_cot, "head", split_axis=0, concat_axis=0, tiled=True)
    for head_slot in range(local_heads):
        pieces, live_use, gather_order, landing, used_blocks = prepared[head_slot]
        cot_rows = pick_rows(recv_cot, head_slot)
        qgrad, kgrad, vgrad, sink_term = backward_head(
            pieces[0],
            pieces[1],
            pieces[2],
            cot_rows,
            head_outs[head_slot],
            lse_list[head_slot],
            live_use,
            sink_logits[head_slot],
            used_blocks,
            BLOCK,
        )
        qgrad_list.append(restore(qgrad, devices))
        kgrad_list.append(restore(kgrad, devices))
        vgrad_list.append(restore(vgrad, devices))
        sink_list.append(sink_term)
    back_qgrad, back_kgrad, back_vgrad = (
        lax.all_to_all(
            jnp.stack(qgrad_list, axis=1), "head", split_axis=0, concat_axis=0, tiled=True
        ),
        lax.all_to_all(
            jnp.stack(kgrad_list, axis=1), "head", split_axis=0, concat_axis=0, tiled=True
        ),
        lax.all_to_all(
            jnp.stack(vgrad_list, axis=1), "head", split_axis=0, concat_axis=0, tiled=True
        ),
    )
    sink_grad = lax.psum(jnp.stack(sink_list), "dp")
    token_out = collect(back_out).astype(jnp.float32)
    mixed = (gate_probs[:, :, None] * token_out).astype(jnp.bfloat16)
    gate_sum = jnp.sum(out_grad[0].astype(jnp.float32) * token_out, axis=-1)
    gate_grad = gate_probs * (gate_sum - jnp.sum(gate_probs * gate_sum, axis=-1, keepdims=True))
    return (
        mixed[None],
        collect(back_qgrad)[None],
        collect(back_kgrad)[None],
        collect(back_vgrad)[None],
        gate_grad[None],
        sink_grad,
    )


def solution(mesh):
    placed = (
        P("dp", "head", None),
        P("dp", "head", None, None),
        P("dp", "head", None, None),
        P("dp", "head", None, None),
        P("dp", "head", None),
        P("head"),
        P("dp", "head", None, None),
    )
    return jax.shard_map(
        per_device,
        mesh=mesh,
        in_specs=placed,
        out_specs=(
            P("dp", "head", None, None),
            P("dp", "head", None, None),
            P("dp", "head", None, None),
            P("dp", "head", None, None),
            P("dp", "head", None),
            P("head"),
        ),
        check_vma=False,
    )
```

profile of v0, /device:TPU:11, one launch (start us, length us, event | category | flops | bytes accessed | tf_op | source)
XLA Modules:
  0.0 202.2 jit_solution(5614113830701706993)
XLA Ops:
  0.7 0.8 broadcast_multiply_fusion
  2.3 7.6 %scatter_custom_fusion = bf16[2048]{0:T(1024)(128)(2,1)S(1)} fusion(s32[1024]{0:T(1024)S(1)} %bitcast.236, bf16[1024]{0:T(1024)(128)(2,1)S(1)} %broadcast.376, bf16[]{:T(256)} %constant.402.clone.1), kind=kCustom, calls=%fused_computation.130 | custom fusion | bytes 4098 | tf_op jit(solution)/shard_map/scatter | solution.py:211
  9.9 0.7 reshape.293
  10.6 6.5 %all-to-all-start = ((bf16[16,4,32]{2,1,0:T(4,128)(2,1)}), bf16[16,4,32]{2,1,0:T(4,128)(2,1)S(1)}, u32[]{:S(2)}, u32[]{:S(2)}) async-start(bf16[16,4,32]{2,1,0:T(4,128)(2,1)} %reshape.293), calls=%async_computation | async-start | bytes 32768 | tf_op jit(solution)/shard_map/all_to_all | solution.py:219
  17.1 4.0 %scatter_custom_fusion.2 = bf16[2048,128]{1,0:T(8,128)(2,1)} fusion(s32[1024]{0:T(1024)S(1)} %bitcast.237, bf16[1,128,8,128]{3,2,1,0:T(8,128)(2,1)S(1)} %copy-done, bf16[]{:T(256)} %constant.402.clone.1), kind=kCustom, calls=%fused_computation.91 | custom fusion | bytes 786434 | tf_op jit(solution)/shard_map/scatter | solution.py:193
  21.2 6.0 %all-to-all-start.2 = ((bf16[16,4,32,128]{3,2,1,0:T(8,128)(2,1)}), bf16[16,4,32,128]{3,2,1,0:T(8,128)(2,1)S(1)}, u32[]{:S(2)}, u32[]{:S(2)}) async-start(bf16[16,4,32,128]{3,2,1,0:T(8,128)(2,1)} %bitcast.7), calls=%async_computation.2 | async-start | bytes 1048576 | tf_op jit(solution)/shard_map/all_to_all | solution.py:217
  27.2 4.0 %scatter_custom_fusion.1 = bf16[2048,128]{1,0:T(8,128)(2,1)} fusion(s32[1024]{0:T(1024)S(1)} %bitcast.238, bf16[1,128,8,128]{3,2,1,0:T(8,128)(2,1)S(1)} %copy-done.18, bf16[]{:T(256)} %constant.402.clone.1), kind=kCustom, calls=%fused_computation.93 | custom fusion | bytes 786434 | tf_op jit(solution)/shard_map/scatter | solution.py:193
  31.2 9.6 %all-to-all-done.2 = bf16[16,4,32,128]{3,2,1,0:T(8,128)(2,1)S(1)} async-done(((bf16[16,4,32,128]{3,2,1,0:T(8,128)(2,1)}), bf16[16,4,32,128]{3,2,1,0:T(8,128)(2,1)S(1)}, u32[]{:S(2)}, u32[]{:S(2)}) %all-to-all-start.2) | async-done | bytes 524320 | tf_op jit(solution)/shard_map/all_to_all | solution.py:217
  40.8 5.0 %all-to-all-start.1 = ((bf16[16,4,32,128]{3,2,1,0:T(8,128)(2,1)}), bf16[16,4,32,128]{3,2,1,0:T(8,128)(2,1)S(1)}, u32[]{:S(2)}, u32[]{:S(2)}) async-start(bf16[16,4,32,128]{3,2,1,0:T(8,128)(2,1)} %bitcast.4), calls=%async_computation.1 | async-start | bytes 1048576 | tf_op jit(solution)/shard_map/all_to_all | solution.py:216
  46.8 4.5 %scatter_custom_fusion.4 = bf16[2048,128]{1,0:T(8,128)(2,1)} fusion(s32[1024]{0:T(1024)S(1)} %bitcast.239, bf16[1,128,8,128]{3,2,1,0:T(8,128)(2,1)S(1)} %copy-done.4, f32[1024]{0:T(1024)S(1)} %exponential_divide_fusion, bf16[]{:T(256)} %constant.402.clone.1), kind=kCustom, calls=%fused_computation.88 | custom fusion | flops 393216 | bytes 790530 | tf_op jit(solution)/shard_map/scatter | solution.py:193
  51.2 8.1 %all-to-all-done.1 = bf16[16,4,32,128]{3,2,1,0:T(8,128)(2,1)S(1)} async-done(((bf16[16,4,32,128]{3,2,1,0:T(8,128)(2,1)}), bf16[16,4,32,128]{3,2,1,0:T(8,128)(2,1)S(1)}, u32[]{:S(2)}, u32[]{:S(2)}) %all-to-all-start.1) | async-done | bytes 524320 | tf_op jit(solution)/shard_map/all_to_all | solution.py:216
  59.4 5.0 %all-to-all-start.5 = ((bf16[16,4,32,128]{3,2,1,0:T(8,128)(2,1)}), bf16[16,4,32,128]{3,2,1,0:T(8,128)(2,1)S(1)}, u32[]{:S(2)}, u32[]{:S(2)}) async-start(bf16[16,4,32,128]{3,2,1,0:T(8,128)(2,1)} %bitcast.36), calls=%async_computation.5 | async-start | bytes 1048576 | tf_op jit(solution)/shard_map/all_to_all | solution.py:250
  64.4 4.0 %scatter_custom_fusion.3 = bf16[2048,128]{1,0:T(8,128)(2,1)} fusion(s32[1024]{0:T(1024)S(1)} %bitcast.240, bf16[1,128,8,128]{3,2,1,0:T(8,128)(2,1)S(1)} %copy-done.19, bf16[]{:T(256)} %constant.402.clone.1), kind=kCustom, calls=%fused_computation.89 | custom fusion | bytes 786434 | tf_op jit(solution)/shard_map/scatter | solution.py:193
  68.4 0.6 fusion.66
  69.5 0.7 fusion.63
  70.2 0.8 fusion.64
  71.4 6.6 %all-to-all-done.5 = bf16[16,4,32,128]{3,2,1,0:T(8,128)(2,1)S(1)} async-done(((bf16[16,4,32,128]{3,2,1,0:T(8,128)(2,1)}), bf16[16,4,32,128]{3,2,1,0:T(8,128)(2,1)S(1)}, u32[]{:S(2)}, u32[]{:S(2)}) %all-to-all-start.5) | async-done | bytes 524320 | tf_op jit(solution)/shard_map/all_to_all | solution.py:250
  78.0 4.9 %all-to-all-start.3 = ((bf16[16,4,32,128]{3,2,1,0:T(8,128)(2,1)}), bf16[16,4,32,128]{3,2,1,0:T(8,128)(2,1)S(1)}, u32[]{:S(2)}, u32[]{:S(2)}) async-start(bf16[16,4,32,128]{3,2,1,0:T(8,128)(2,1)} %bitcast.11), calls=%async_computation.3 | async-start | bytes 1048576 | tf_op jit(solution)/shard_map/all_to_all | solution.py:218
  82.8 0.6 broadcast_maximum_fusion
  83.7 0.6 log_add_fusion
  84.3 0.7 fusion.62
  85.3 11.1 %all-to-all-done.3 = bf16[16,4,32,128]{3,2,1,0:T(8,128)(2,1)S(1)} async-done(((bf16[16,4,32,128]{3,2,1,0:T(8,128)(2,1)}), bf16[16,4,32,128]{3,2,1,0:T(8,128)(2,1)S(1)}, u32[]{:S(2)}, u32[]{:S(2)}) %all-to-all-start.3) | async-done | bytes 524320 | tf_op jit(solution)/shard_map/all_to_all | solution.py:218
  96.4 0.7 fusion.65
  97.1 1.1 multiply_reduce_fusion
  98.6 0.9 fusion.15
  99.9 0.7 broadcast_maximum_fusion.3
  100.8 0.7 log_add_fusion.3
  101.9 1.1 multiply_reduce_fusion.3
  103.0 1.3 fusion.7
  104.2 0.9 fusion.12
  105.5 0.7 broadcast_maximum_fusion.1
  106.5 0.7 log_add_fusion.1
  107.5 1.1 multiply_reduce_fusion.1
  110.0 0.7 broadcast_maximum_fusion.2
  111.0 0.7 log_add_fusion.2
  112.0 0.9 pad_maximum_fusion.3
  112.9 4.9 %all-to-all-start.8 = ((bf16[16,4,32,128]{3,2,1,0:T(8,128)(2,1)}), bf16[16,4,32,128]{3,2,1,0:T(8,128)(2,1)S(1)}, u32[]{:S(2)}, u32[]{:S(2)}) async-start(bf16[16,4,32,128]{3,2,1,0:T(8,128)(2,1)} %pad_maximum_fusion.3), calls=%async_computation.8 | async-start | bytes 1048576 | tf_op jit(solution)/shard_map/all_to_all | solution.py:277
  117.7 1.2 fusion.14
  119.0 1.1 multiply_reduce_fusion.2
  120.1 1.6 fusion.6
  122.1 0.7 copy-done.16
  122.9 0.9 pad_maximum_fusion.2
  123.8 7.5 %all-to-all-done.8 = bf16[16,4,32,128]{3,2,1,0:T(8,128)(2,1)S(1)} async-done(((bf16[16,4,32,128]{3,2,1,0:T(8,128)(2,1)}), bf16[16,4,32,128]{3,2,1,0:T(8,128)(2,1)S(1)}, u32[]{:S(2)}, u32[]{:S(2)}) %all-to-all-start.8) | async-done | bytes 524320 | tf_op jit(solution)/shard_map/all_to_all | solution.py:277
  131.3 4.9 %all-to-all-start.7 = ((bf16[16,4,32,128]{3,2,1,0:T(8,128)(2,1)}), bf16[16,4,32,128]{3,2,1,0:T(8,128)(2,1)S(1)}, u32[]{:S(2)}, u32[]{:S(2)}) async-start(bf16[16,4,32,128]{3,2,1,0:T(8,128)(2,1)} %pad_maximum_fusion.2), calls=%async_computation.7 | async-start | bytes 1048576 | tf_op jit(solution)/shard_map/all_to_all | solution.py:274
  136.2 0.9 pad_maximum_fusion
  137.1 12.7 %all-to-all-done.7 = bf16[16,4,32,128]{3,2,1,0:T(8,128)(2,1)S(1)} async-done(((bf16[16,4,32,128]{3,2,1,0:T(8,128)(2,1)}), bf16[16,4,32,128]{3,2,1,0:T(8,128)(2,1)S(1)}, u32[]{:S(2)}, u32[]{:S(2)}) %all-to-all-start.7) | async-done | bytes 524320 | tf_op jit(solution)/shard_map/all_to_all | solution.py:274
  149.7 4.9 %all-to-all-start.4 = ((bf16[16,4,32,128]{3,2,1,0:T(8,128)(2,1)}), bf16[16,4,32,128]{3,2,1,0:T(8,128)(2,1)S(1)}, u32[]{:S(2)}, u32[]{:S(2)}) async-start(bf16[16,4,32,128]{3,2,1,0:T(8,128)(2,1)} %pad_maximum_fusion), calls=%async_computation.4 | async-start | bytes 1048576 | tf_op jit(solution)/shard_map/all_to_all | solution.py:247
  154.6 1.3 fusion.11
  155.9 1.2 multiply_reduce_fusion.5
  157.4 0.5 copy-done.9
  158.4 0.7 copy-done.2
  159.4 0.9 pad_maximum_fusion.1
  160.3 7.9 %all-to-all-done.4 = bf16[16,4,32,128]{3,2,1,0:T(8,128)(2,1)S(1)} async-done(((bf16[16,4,32,128]{3,2,1,0:T(8,128)(2,1)}), bf16[16,4,32,128]{3,2,1,0:T(8,128)(2,1)S(1)}, u32[]{:S(2)}, u32[]{:S(2)}) %all-to-all-start.4) | async-done | bytes 524320 | tf_op jit(solution)/shard_map/all_to_all | solution.py:247
  168.2 4.9 %all-to-all-start.6 = ((bf16[16,4,32,128]{3,2,1,0:T(8,128)(2,1)}), bf16[16,4,32,128]{3,2,1,0:T(8,128)(2,1)S(1)}, u32[]{:S(2)}, u32[]{:S(2)}) async-start(bf16[16,4,32,128]{3,2,1,0:T(8,128)(2,1)} %pad_maximum_fusion.1), calls=%async_computation.6 | async-start | bytes 1048576 | tf_op jit(solution)/shard_map/all_to_all | solution.py:271
  173.1 1.3 multiply_reduce_fusion.8
  175.6 1.3 multiply_reduce_fusion.6
  177.5 1.3 multiply_reduce_fusion.7
  179.5 4.6 %psum.7 = f32[4]{0:T(128)} all-reduce(f32[4]{0:T(128)S(1)} %pad_maximum_fusion.4), channel_id=1, replica_groups=mesh['dp'=2,'head'=16] {'dp'}, use_global_device_ids=true, to_apply=%region_28.29 | all-reduce | flops 4 | bytes 32 | tf_op jit(solution)/shard_map/psum | solution.py:281
  184.1 4.3 %gather_fusion.3 = bf16[1024,128]{1,0:T(8,128)(2,1)} fusion(bf16[2048,128]{1,0:T(8,128)(2,1)S(1)} %bitcast.179, s32[1024]{0:T(1024)S(1)} %broadcast_clamp_fusion), kind=kCustom, calls=%fused_computation.3 | custom fusion | bytes 528384 | tf_op jit(solution)/shard_map/gather | solution.py:198
  188.4 4.3 %gather_fusion.2 = bf16[1024,128]{1,0:T(8,128)(2,1)} fusion(bf16[2048,128]{1,0:T(8,128)(2,1)S(1)} %bitcast.180, s32[1024]{0:T(1024)S(1)} %broadcast_clamp_fusion), kind=kCustom, calls=%fused_computation.2 | custom fusion | bytes 528384 | tf_op jit(solution)/shard_map/gather | solution.py:198
  192.7 3.2 %gather_fusion = bf16[1024,128]{1,0:T(8,128)(2,1)S(1)} fusion(bf16[2048,128]{1,0:T(8,128)(2,1)S(1)} %bitcast.181, s32[1024]{0:T(1024)S(1)} %broadcast_clamp_fusion), kind=kCustom, calls=%fused_computation | custom fusion | bytes 528384 | tf_op jit(solution)/shard_map/gather | solution.py:198
  196.4 4.3 %gather_fusion.1 = bf16[1024,128]{1,0:T(8,128)(2,1)} fusion(bf16[2048,128]{1,0:T(8,128)(2,1)S(1)} %bitcast.182, s32[1024]{0:T(1024)S(1)} %broadcast_clamp_fusion), kind=kCustom, calls=%fused_computation.1 | custom fusion | bytes 528384 | tf_op jit(solution)/shard_map/gather | solution.py:198
  200.7 0.9 fusion.25
  201.6 0.6 fusion.50
  (110 shorter events, 9.8 us)
Async XLA Ops:
  0.6 16.5 %copy-start = (bf16[1,128,8,128]{3,2,1,0:T(8,128)(2,1)S(1)}, bf16[1,128,8,128]{3,2,1,0:T(8,128)(2,1)}, u32[]{:S(2)}) copy-start(bf16[1,128,8,128]{3,2,1,0:T(8,128)(2,1)} %param.9) | copy-start | bytes 786436
  0.6 0.8 copy-start.29
  10.6 10.7 %all-to-all-start = ((bf16[16,4,32]{2,1,0:T(4,128)(2,1)}), bf16[16,4,32]{2,1,0:T(4,128)(2,1)S(1)}, u32[]{:S(2)}, u32[]{:S(2)}) async-start(bf16[16,4,32]{2,1,0:T(4,128)(2,1)} %reshape.293), calls=%async_computation | async-start | bytes 32768 | tf_op jit(solution)/shard_map/all_to_all | solution.py:219
  21.2 6.0 %copy-start.18 = (bf16[1,128,8,128]{3,2,1,0:T(8,128)(2,1)S(1)}, bf16[1,128,8,128]{3,2,1,0:T(8,128)(2,1)}, u32[]{:S(2)}) copy-start(bf16[1,128,8,128]{3,2,1,0:T(8,128)(2,1)} %param.8) | copy-start | bytes 786436
  21.2 19.6 %all-to-all-start.2 = ((bf16[16,4,32,128]{3,2,1,0:T(8,128)(2,1)}), bf16[16,4,32,128]{3,2,1,0:T(8,128)(2,1)S(1)}, u32[]{:S(2)}, u32[]{:S(2)}) async-start(bf16[16,4,32,128]{3,2,1,0:T(8,128)(2,1)} %bitcast.7), calls=%async_computation.2 | async-start | bytes 1048576 | tf_op jit(solution)/shard_map/all_to_all | solution.py:217
  40.8 5.0 %copy-start.28 = (f32[1,128,8]{1,2,0:T(8,128)S(1)}, f32[1,128,8]{1,2,0:T(8,128)}, u32[]{:S(2)}) copy-start(f32[1,128,8]{1,2,0:T(8,128)} %param.11) | copy-start | bytes 12292
  40.8 18.6 %all-to-all-start.1 = ((bf16[16,4,32,128]{3,2,1,0:T(8,128)(2,1)}), bf16[16,4,32,128]{3,2,1,0:T(8,128)(2,1)S(1)}, u32[]{:S(2)}, u32[]{:S(2)}) async-start(bf16[16,4,32,128]{3,2,1,0:T(8,128)(2,1)} %bitcast.4), calls=%async_computation.1 | async-start | bytes 1048576 | tf_op jit(solution)/shard_map/all_to_all | solution.py:216
  45.8 1.0 copy-start.4
  59.4 5.0 %copy-start.19 = (bf16[1,128,8,128]{3,2,1,0:T(8,128)(2,1)S(1)}, bf16[1,128,8,128]{3,2,1,0:T(8,128)(2,1)}, u32[]{:S(2)}) copy-start(bf16[1,128,8,128]{3,2,1,0:T(8,128)(2,1)} %param.10) | copy-start | bytes 786436
  59.4 18.6 %all-to-all-start.5 = ((bf16[16,4,32,128]{3,2,1,0:T(8,128)(2,1)}), bf16[16,4,32,128]{3,2,1,0:T(8,128)(2,1)S(1)}, u32[]{:S(2)}, u32[]{:S(2)}) async-start(bf16[16,4,32,128]{3,2,1,0:T(8,128)(2,1)} %bitcast.36), calls=%async_computation.5 | async-start | bytes 1048576 | tf_op jit(solution)/shard_map/all_to_all | solution.py:250
  64.4 4.0 %copy-start.30 = (f32[4]{0:T(128)S(1)}, f32[4]{0:T(128)}, u32[]{:S(2)}) copy-start(f32[4]{0:T(128)} %param.12) | copy-start | bytes 52
  70.2 0.8 copy-start.12
  70.2 29.3 %copy-start.10 = (bf16[16,1,32,128]{3,2,1,0:T(8,128)(2,1)}, bf16[16,1,32,128]{3,2,1,0:T(8,128)(2,1)S(1)}, u32[]{:S(2)}) copy-start(bf16[16,1,32,128]{3,2,1,0:T(8,128)(2,1)S(1)} %get-tuple-element.1312) | copy-start | bytes 393220
  70.2 34.9 %copy-start.8 = (bf16[16,1,32,128]{3,2,1,0:T(8,128)(2,1)}, bf16[16,1,32,128]{3,2,1,0:T(8,128)(2,1)S(1)}, u32[]{:S(2)}) copy-start(bf16[16,1,32,128]{3,2,1,0:T(8,128)(2,1)S(1)} %get-tuple-element.1314) | copy-start | bytes 393220
  71.0 34.1 %copy-start.15 = (bf16[16,1,32,128]{3,2,1,0:T(8,128)(2,1)}, bf16[16,1,32,128]{3,2,1,0:T(8,128)(2,1)S(1)}, u32[]{:S(2)}) copy-start(bf16[16,1,32,128]{3,2,1,0:T(8,128)(2,1)S(1)} %get-tuple-element.1318) | copy-start | bytes 393220
  78.0 18.4 %all-to-all-start.3 = ((bf16[16,4,32,128]{3,2,1,0:T(8,128)(2,1)}), bf16[16,4,32,128]{3,2,1,0:T(8,128)(2,1)S(1)}, u32[]{:S(2)}, u32[]{:S(2)}) async-start(bf16[16,4,32,128]{3,2,1,0:T(8,128)(2,1)} %bitcast.11), calls=%async_computation.3 | async-start | bytes 1048576 | tf_op jit(solution)/shard_map/all_to_all | solution.py:218
  85.0 16.9 %copy-start.26 = (bf16[16,1,32,128]{3,2,1,0:T(8,128)(2,1)}, bf16[16,1,32,128]{3,2,1,0:T(8,128)(2,1)S(1)}, u32[]{:S(2)}) copy-start(bf16[16,1,32,128]{3,2,1,0:T(8,128)(2,1)S(1)} %get-tuple-element.1308) | copy-start | bytes 393220
  108.6 0.9 copy-start.6
  108.6 1.0 copy-start.13
  109.9 9.0 %copy-start.3 = (f32[512,512]{0,1:T(8,128)}, f32[512,512]{0,1:T(8,128)S(1)}, u32[]{:S(2)}) copy-start(f32[512,512]{0,1:T(8,128)S(1)} %get-tuple-element.1333) | copy-start | bytes 3145732
  110.6 1.0 copy-start.21
  112.9 18.4 %all-to-all-start.8 = ((bf16[16,4,32,128]{3,2,1,0:T(8,128)(2,1)}), bf16[16,4,32,128]{3,2,1,0:T(8,128)(2,1)S(1)}, u32[]{:S(2)}, u32[]{:S(2)}) async-start(bf16[16,4,32,128]{3,2,1,0:T(8,128)(2,1)} %pad_maximum_fusion.3), calls=%async_computation.8 | async-start | bytes 1048576 | tf_op jit(solution)/shard_map/all_to_all | solution.py:277
  117.7 1.3 copy-start.22
  117.7 1.3 copy-start.24
  120.1 1.6 copy-start.14
  121.8 2.0 %copy-start.1 = (bf16[512,512]{0,1:T(8,128)(2,1)}, bf16[512,512]{0,1:T(8,128)(2,1)S(1)}, u32[]{:S(2)}) copy-start(bf16[512,512]{0,1:T(8,128)(2,1)S(1)} %fusion.6) | copy-start | bytes 1572868
  121.8 1.0 copy-start.16
  121.8 1.1 copy-start.17
  123.8 12.4 %copy-start.20 = (bf16[512,128]{1,0:T(8,128)(2,1)S(1)}, bf16[512,128]{1,0:T(8,128)(2,1)}, u32[]{:S(2)}) copy-start(bf16[512,128]{1,0:T(8,128)(2,1)} %get-tuple-element.1337) | copy-start | bytes 393220
  123.8 12.4 %copy-start.23 = (bf16[512,128]{1,0:T(8,128)(2,1)S(1)}, bf16[512,128]{1,0:T(8,128)(2,1)}, u32[]{:S(2)}) copy-start(bf16[512,128]{1,0:T(8,128)(2,1)} %get-tuple-element.1343) | copy-start | bytes 393220
  123.8 12.4 %copy-start.25 = (bf16[512,128]{1,0:T(8,128)(2,1)S(1)}, bf16[512,128]{1,0:T(8,128)(2,1)}, u32[]{:S(2)}) copy-start(bf16[512,128]{1,0:T(8,128)(2,1)} %get-tuple-element.1339) | copy-start | bytes 393220
  123.8 12.4 %copy-start.27 = (bf16[512,128]{1,0:T(8,128)(2,1)S(1)}, bf16[512,128]{1,0:T(8,128)(2,1)}, u32[]{:S(2)}) copy-start(bf16[512,128]{1,0:T(8,128)(2,1)} %get-tuple-element.1341) | copy-start | bytes 393220
  131.3 18.4 %all-to-all-start.7 = ((bf16[16,4,32,128]{3,2,1,0:T(8,128)(2,1)}), bf16[16,4,32,128]{3,2,1,0:T(8,128)(2,1)S(1)}, u32[]{:S(2)}, u32[]{:S(2)}) async-start(bf16[16,4,32,128]{3,2,1,0:T(8,128)(2,1)} %pad_maximum_fusion.2), calls=%async_computation.7 | async-start | bytes 1048576 | tf_op jit(solution)/shard_map/all_to_all | solution.py:274
  149.7 18.4 %all-to-all-start.4 = ((bf16[16,4,32,128]{3,2,1,0:T(8,128)(2,1)}), bf16[16,4,32,128]{3,2,1,0:T(8,128)(2,1)S(1)}, u32[]{:S(2)}, u32[]{:S(2)}) async-start(bf16[16,4,32,128]{3,2,1,0:T(8,128)(2,1)} %pad_maximum_fusion), calls=%async_computation.4 | async-start | bytes 1048576 | tf_op jit(solution)/shard_map/all_to_all | solution.py:247
  154.6 2.5 %copy-start.11 = (bf16[16,1,32,128]{3,2,1,0:T(8,128)(2,1)S(1)}, bf16[16,1,32,128]{3,2,1,0:T(8,128)(2,1)}, u32[]{:S(2)}) copy-start(bf16[16,1,32,128]{3,2,1,0:T(8,128)(2,1)} %copy-done.10) | copy-start | bytes 393220
  157.1 0.9 copy-start.9
  158.0 1.0 copy-start.2
  158.0 1.1 copy-start.7
  168.2 28.2 %all-to-all-start.6 = ((bf16[16,4,32,128]{3,2,1,0:T(8,128)(2,1)}), bf16[16,4,32,128]{3,2,1,0:T(8,128)(2,1)S(1)}, u32[]{:S(2)}, u32[]{:S(2)}) async-start(bf16[16,4,32,128]{3,2,1,0:T(8,128)(2,1)} %pad_maximum_fusion.1), calls=%async_computation.6 | async-start | bytes 1048576 | tf_op jit(solution)/shard_map/all_to_all | solution.py:271
  192.7 3.2 %copy-start.5 = (bf16[1,128,8,128]{3,2,1,0:T(8,128)(2,1)S(1)}, bf16[1,128,8,128]{3,2,1,0:T(8,128)(2,1)}, u32[]{:S(2)}) copy-start(bf16[1,128,8,128]{3,2,1,0:T(8,128)(2,1)} %param.13) | copy-start | bytes 786436
where the time goes:
time: 205 us; the launch traced here: 202 us
  waiting for transfers between devices  63.6 us (31%)
  starting transfers between devices  46.8 us (23%)
  local copies, waits for them, and re-layouts  44.4 us (22%)
  other arithmetic  22.6 us (11%)
  matrix products  16.5 us (8%)
  blocking collectives  4.56 us (2%)
  between operations  3.7 us (2%)
    gather x4, local copies, waits for them, and re-layouts, collect(): buffer.reshape(buffer_rows, buffer.shape[-1])[target]  16.1 us
    all_to_all x1, waiting for transfers between devices, per_device(): lax.all_to_all(jnp.stack(kgrad_list, axis=1), 'head', split_axis=0, conca...  12.7 us
    scatter x3, local copies, waits for them, and re-layouts, spread_out(): jnp.zeros((buffer_rows, flat_rows.shape[-1]), flat_rows.dtype).at[target]  12 us
    all_to_all x1, waiting for transfers between devices, per_device(): lax.all_to_all(send_value, 'head', split_axis=0, concat_axis=0, tiled=True)  11.1 us
    all_to_all x1, waiting for transfers between devices, per_device(): lax.all_to_all(send_key, 'head', split_axis=0, concat_axis=0, tiled=True)  9.59 us
    all_to_all x1, waiting for transfers between devices, per_device(): lax.all_to_all(send_query, 'head', split_axis=0, concat_axis=0, tiled=True)  8.15 us
    all_to_all x1, waiting for transfers between devices, per_device(): lax.all_to_all(jnp.stack(out_list, axis=1), 'head', split_axis=0, concat_...  7.93 us
    scatter x1, local copies, waits for them, and re-layouts, per_device(): filled = jnp.zeros((buffer_rows,), jnp.bfloat16).at[target].set(jnp.ones(...  7.59 us
  transfers between devices with their start and end apart: 9, of which 8 were waited for; matrix products, arithmetic and copies ran while one was open for 24% of the time, Pallas kernels for 0%

commit v1 on v0

v1 whole, which is shorter than its diff:
```python
import functools
import math

import jax
import jax.numpy as jnp
from jax import lax
from jax.experimental import pallas as pl
from jax.experimental.pallas import tpu as pltpu
from jax.sharding import PartitionSpec as P

SLOT = 32
INFO = 16
MASKED = -1e30


def dot(a, b, dims):
    return lax.dot_general(a, b, (dims, ((), ())), preferred_element_type=jnp.float32)


def pack_kernel(heads, local_heads, dests, ids_ref, q_ref, k_ref, v_ref, c_ref, out_ref, target_ref, count_ref):
    step = pl.program_id(0)
    rows = ids_ref.shape[1]
    width = local_heads * SLOT

    @pl.when(step == 0)
    def _():
        lower = lax.broadcasted_iota(jnp.int32, (128, 128), 0)
        upper = lax.broadcasted_iota(jnp.int32, (128, 128), 1)
        before = jnp.where(lower < upper, 1.0, 0.0).astype(jnp.bfloat16)
        running = jnp.zeros((heads, 1), jnp.float32)
        for start in range(0, rows, 128):
            ids = ids_ref[:, start : start + 128]
            named = jnp.where(lax.broadcasted_iota(jnp.int32, (heads, 128), 0) == ids, 1.0, 0.0)
            earlier = dot(named.astype(jnp.bfloat16), before, ((1,), (0,))) + running
            place = jnp.sum(named * earlier, axis=0, keepdims=True)
            target_ref[:, start : start + 128] = ids * SLOT + place.astype(jnp.int32)
            running = running + jnp.sum(named, axis=1, keepdims=True)
        count_ref[...] = jnp.broadcast_to(running, (heads, 128))

    chunk = dests * width
    row = lax.broadcasted_iota(jnp.int32, (chunk, rows), 0) + step * chunk
    pick = jnp.where(row == target_ref[...], 1.0, 0.0).astype(jnp.bfloat16)
    for pair, refs in enumerate(((q_ref, k_ref), (v_ref, c_ref))):
        both = jnp.concatenate([refs[0][...], refs[1][...]], axis=1)
        res = dot(pick, both, ((1,), (0,))).astype(jnp.bfloat16)
        for part in range(2):
            start = (2 * pair + part) * width
            out_ref[:, start : start + width, :] = res[:, part * 128 : part * 128 + 128].reshape(dests, width, 128)
    line = lax.broadcasted_iota(jnp.int32, (dests * INFO, heads), 0)
    head = lax.broadcasted_iota(jnp.int32, (dests * INFO, heads), 1)
    wanted = (step * dests + line // INFO) * local_heads + line % INFO
    take = jnp.where((wanted == head) & (line % INFO < local_heads), 1.0, 0.0).astype(jnp.bfloat16)
    info = dot(take, count_ref[...].astype(jnp.bfloat16), ((1,), (0,)))
    out_ref[:, 4 * width :, :] = info.astype(jnp.bfloat16).reshape(dests, INFO, 128)


def attend_kernel(local_heads, block, sink_ref, recv_ref, out_ref, term_ref, dk_ref, dv_ref):
    head = pl.program_id(0)
    devices = recv_ref.shape[0]
    width = local_heads * SLOT
    rows = devices * SLOT
    depth = recv_ref.shape[-1]
    scale = 1.0 / math.sqrt(depth)
    sink = sink_ref[head]

    def part(index, first, size):
        start = pl.multiple_of(index * width + head * SLOT, SLOT)
        begin, count = first // SLOT, size // SLOT
        return recv_ref[begin : begin + count, pl.ds(start, SLOT), :].reshape(size, depth)

    def put(index, first, value):
        start = pl.multiple_of(index * width + head * SLOT, SLOT)
        begin, count = first // SLOT, value.shape[0] // SLOT
        out_ref[begin : begin + count, pl.ds(start, SLOT), :] = value.reshape(count, SLOT, depth)

    info = recv_ref[:, 4 * width :, :].astype(jnp.float32)
    line = lax.broadcasted_iota(jnp.int32, info.shape, 1)
    count = jnp.sum(jnp.where(line == head, info, 0.0), axis=1, keepdims=True)
    slot = lax.broadcasted_iota(jnp.int32, (devices, SLOT, 128), 1).astype(jnp.float32)
    dead = jnp.where(slot < count, 0.0, MASKED).reshape(rows, 128)

    below = lax.broadcasted_iota(jnp.int32, (block, block), 0) <= lax.broadcasted_iota(jnp.int32, (block, block), 1)
    blocks = rows // block
    total = jnp.zeros((1, block), jnp.float32)
    for qb in range(blocks):
        query = part(0, qb * block, block)
        cot = part(3, qb * block, block)
        scores = []
        top = jnp.full((1, block), sink, jnp.float32)
        for kb in range(qb + 1):
            key = part(1, kb * block, block)
            bias = jnp.concatenate([dead[kb * block : (kb + 1) * block]] * (block // 128), axis=1)
            score = scale * dot(key, query, ((1,), (1,))) + bias
            if kb == qb:
                score = jnp.where(below, score, MASKED)
            scores.append(score)
            top = jnp.maximum(top, jnp.max(score, axis=0, keepdims=True))
        sink_part = jnp.exp(sink - top)
        run = sink_part
        for kb in range(qb + 1):
            scores[kb] = jnp.exp(scores[kb] - top)
            run = run + jnp.sum(scores[kb], axis=0, keepdims=True)
        inv = 1.0 / run
        head_out = jnp.zeros((depth, block), jnp.float32)
        delta = jnp.zeros((1, block), jnp.float32)
        terms = []
        for kb in range(qb + 1):
            value = part(2, kb * block, block)
            prob = scores[kb] * inv
            weights = prob.astype(jnp.bfloat16)
            head_out = head_out + dot(value, weights, ((0,), (0,)))
            vpart = dot(weights, cot, ((1,), (0,)))
            dv_ref[kb * block : (kb + 1) * block] = vpart if kb == qb else dv_ref[kb * block : (kb + 1) * block] + vpart
            term = prob * dot(value, cot, ((1,), (1,)))
            delta = delta + jnp.sum(term, axis=0, keepdims=True)
            scores[kb] = prob
            terms.append(term)
        put(0, qb * block, head_out.T.astype(jnp.bfloat16))
        query_grad = jnp.zeros((depth, block), jnp.float32)
        for kb in range(qb + 1):
            dscore = (terms[kb] - scores[kb] * delta).astype(jnp.bfloat16)
            query_grad = query_grad + dot(part(1, kb * block, block), dscore, ((0,), (0,)))
            kpart = dot(dscore, query, ((1,), (0,)))
            dk_ref[kb * block : (kb + 1) * block] = kpart if kb == qb else dk_ref[kb * block : (kb + 1) * block] + kpart
        put(1, qb * block, (scale * query_grad).T.astype(jnp.bfloat16))
        total = total - sink_part * inv * delta
    for kb in range(blocks):
        put(2, kb * block, (scale * dk_ref[kb * block : (kb + 1) * block]).astype(jnp.bfloat16))
        put(3, kb * block, dv_ref[kb * block : (kb + 1) * block].astype(jnp.bfloat16))
    term_ref[0] = jnp.broadcast_to(jnp.sum(total, axis=1, keepdims=True), (8, 128))


def unpack_kernel(width, target_ref, gate_ref, grad_ref, back_ref, mixed_ref, dq_ref, dk_ref, dv_ref, sum_ref):
    chunk = target_ref.shape[0]
    devices = back_ref.shape[0]
    slots = devices * width
    row = lax.broadcasted_iota(jnp.int32, (chunk, slots), 1)
    pick = jnp.where(row == target_ref[...], 1.0, 0.0).astype(jnp.bfloat16)

    def both(first):
        halves = [
            back_ref[:, index * width : (index + 1) * width, :].reshape(slots, 128) for index in (first, first + 1)
        ]
        return dot(pick, jnp.concatenate(halves, axis=1), ((1,), (0,)))

    forward = both(0)
    token_out = forward[:, :128]
    mixed_ref[...] = (gate_ref[...] * token_out).astype(jnp.bfloat16)
    sum_ref[...] = jnp.sum(grad_ref[...].astype(jnp.float32) * token_out, axis=1, keepdims=True)
    dq_ref[...] = forward[:, 128:].astype(jnp.bfloat16)
    backward = both(2)
    dk_ref[...] = backward[:, :128].astype(jnp.bfloat16)
    dv_ref[...] = backward[:, 128:].astype(jnp.bfloat16)


def per_device(head_ids, query_slots, key_slots, value_slots, gate_logits, sink_logits, out_grad):
    devices = lax.axis_size("head")
    local_heads = sink_logits.shape[0]
    heads = local_heads * devices
    tokens, slots = head_ids.shape[1:]
    depth = query_slots.shape[-1]
    rows = tokens * slots
    width = local_heads * SLOT
    ids = head_ids.reshape(1, rows)
    gate_probs = jax.nn.softmax(gate_logits[0], axis=-1)
    cotangent = (gate_probs[:, :, None] * out_grad[0].astype(jnp.float32)).astype(jnp.bfloat16)
    flat = [item.reshape(rows, depth) for item in (query_slots, key_slots, value_slots, cotangent)]
    dests = max(1, 512 // width)
    message = 4 * width + INFO
    whole = lambda shape: pl.BlockSpec(shape, lambda *_: (0,) * len(shape))
    send, target = pl.pallas_call(
        functools.partial(pack_kernel, heads, local_heads, dests),
        grid=(devices // dests,),
        in_specs=[whole((1, rows))] + [whole((rows, depth))] * 4,
        out_specs=[pl.BlockSpec((dests, message, depth), lambda i: (i, 0, 0)), whole((1, rows))],
        out_shape=[
            jax.ShapeDtypeStruct((devices, message, depth), jnp.bfloat16),
            jax.ShapeDtypeStruct((1, rows), jnp.int32),
        ],
        scratch_shapes=[pltpu.VMEM((heads, 128), jnp.float32)],
        name="pack",
    )(ids, *flat)
    recv = lax.all_to_all(send, "head", split_axis=0, concat_axis=0, tiled=True)
    capacity = devices * SLOT
    block = min(256, capacity)
    result, terms = pl.pallas_call(
        functools.partial(attend_kernel, local_heads, block),
        grid=(local_heads,),
        in_specs=[pl.BlockSpec(memory_space=pltpu.SMEM), whole((devices, message, depth))],
        out_specs=[whole((devices, 4 * width, depth)), pl.BlockSpec((1, 8, 128), lambda i: (i, 0, 0))],
        out_shape=[
            jax.ShapeDtypeStruct((devices, 4 * width, depth), jnp.bfloat16),
            jax.ShapeDtypeStruct((local_heads, 8, 128), jnp.float32),
        ],
        scratch_shapes=[pltpu.VMEM((capacity, depth), jnp.float32)] * 2,
        name="attend",
    )(sink_logits, recv)
    back = lax.all_to_all(result, "head", split_axis=0, concat_axis=0, tiled=True)
    sink_grad = terms[:, 0, 0]
    groups = lax.axis_size("dp")
    mine = sink_grad
    for shift in range(1, groups):
        sink_grad = sink_grad + lax.ppermute(mine, "dp", [(i, (i + shift) % groups) for i in range(groups)])
    chunk = min(512, rows)
    column = pl.BlockSpec((chunk, 1), lambda i: (i, 0))
    matrix = pl.BlockSpec((chunk, depth), lambda i: (i, 0))
    mixed, dq, dk, dv, gate_sum = pl.pallas_call(
        functools.partial(unpack_kernel, width),
        grid=(rows // chunk,),
        in_specs=[column, column, matrix, whole((devices, 4 * width, depth))],
        out_specs=[matrix] * 4 + [column],
        out_shape=[jax.ShapeDtypeStruct((rows, depth), jnp.bfloat16)] * 4
        + [jax.ShapeDtypeStruct((rows, 1), jnp.float32)],
        name="unpack",
    )(target.reshape(rows, 1), gate_probs.reshape(rows, 1), out_grad.reshape(rows, depth), back)
    gate_sum = gate_sum.reshape(tokens, slots)
    gate_grad = gate_probs * (gate_sum - jnp.sum(gate_probs * gate_sum, axis=-1, keepdims=True))
    shape = query_slots.shape
    return (
        mixed.reshape(shape),
        dq.reshape(shape),
        dk.reshape(shape),
        dv.reshape(shape),
        gate_grad[None],
        sink_grad,
    )


def solution(mesh):
    wide, narrow = P("dp", "head", None, None), P("dp", "head", None)
    return jax.shard_map(
        per_device,
        mesh=mesh,
        in_specs=(narrow, wide, wide, wide, narrow, P("head"), wide),
        out_specs=(wide, wide, wide, wide, narrow, P("head")),
        check_vma=False,
    )
```

time: 205 us -> 139 us (0.68)
  blocking collectives: 4.56 us -> 55.4 us
  starting transfers between devices: 46.8 us -> 7.21 us
  local copies, waits for them, and re-layouts: 44.4 us -> 6.77 us
  waiting for transfers between devices: 63.6 us -> 42.2 us
  Pallas kernels: 0 us -> 19.5 us
  matrix products: 16.5 us -> 0 us
  other arithmetic: 22.6 us -> 6.23 us
  between operations: 3.7 us -> 0.71 us
    all_to_all x0 -> x1, blocking collectives: none -> 55.4 us  [per_device(): recv = lax.all_to_all(send, 'head', split_axis=0, concat_axis=0, tiled=True)]
    all_to_all x9 -> x1, starting transfers between devices: 46.8 us -> 5.92 us  [per_device(): lax.all_to_all(result, 'head', split_axis=0, concat_axis=0, tiled=True)]
    all_to_all x9 -> x1, waiting for transfers between devices: 63.6 us -> 40.7 us  [per_device(): lax.all_to_all(result, 'head', split_axis=0, concat_axis=0, tiled=True)]
    scatter x4 -> x0, local copies, waits for them, and re-layouts: 19.6 us -> none  [the longest x3 12 us: spread_out(): jnp.zeros((buffer_rows, flat_rows.shape[-1]), flat_rows.dtype).at[target]]
    pallas_call x0 -> x3, Pallas kernels: none -> 19.5 us  [the longest x1 8.88 us: per_device(): pl.pallas_call(functools.partial(attend_kernel, local_heads, block), grid...]
    dot_general x24 -> x0, matrix products: 16.5 us -> none  [the longest x4 4.4 us: value_step(): jnp.dot(weights, value_tile, preferred_element_type=jnp.float32)]
    gather x4 -> x0, local copies, waits for them, and re-layouts: 16.1 us -> none  [collect(): buffer.reshape(buffer_rows, buffer.shape[-1])[target]]
    reduce_sum x11 -> x0, other arithmetic: 6.45 us -> none  [the longest x4 4.95 us: backward_head(): sink_term = -jnp.sum(jnp.exp(sink_value - lse_all) * deltas)]
  transfers between devices with their start and end apart: 9 -> 2, of which waited for: 8 -> 2; matrix products, arithmetic and copies ran while one was open for 24% -> 3% of each run, Pallas kernels for 0% -> 0%
where the time goes in v1:
time: 139 us; the launch traced here: 138 us
  blocking collectives  55.4 us (40%)
  waiting for transfers between devices  42.2 us (30%)
  Pallas kernels  19.5 us (14%)
  starting transfers between devices  7.21 us (5%)
  local copies, waits for them, and re-layouts  6.77 us (5%)
  other arithmetic  6.23 us (4%)
    all_to_all x1, blocking collectives, per_device(): recv = lax.all_to_all(send, 'head', split_axis=0, concat_axis=0, tiled=True)  55.4 us
    all_to_all x1, waiting for transfers between devices, per_device(): lax.all_to_all(result, 'head', split_axis=0, concat_axis=0, tiled=True)  40.7 us
    pallas_call x1, Pallas kernels, per_device(): pl.pallas_call(functools.partial(attend_kernel, local_heads, block), grid...  8.88 us
    all_to_all x1, starting transfers between devices, per_device(): lax.all_to_all(result, 'head', split_axis=0, concat_axis=0, tiled=True)  5.92 us
    pallas_call x1, Pallas kernels, per_device(): pl.pallas_call(functools.partial(unpack_kernel, width), grid=(rows // chu...  5.46 us
    pallas_call x1, Pallas kernels, per_device(): pl.pallas_call(functools.partial(pack_kernel, heads, local_heads, dests),...  5.2 us
    unnamed x8, local copies, waits for them, and re-layouts  2.94 us
  transfers between devices with their start and end apart: 2, of which 2 were waited for; matrix products, arithmetic and copies ran while one was open for 3% of the time, Pallas kernels for 0%

profile of v1, /device:TPU:11, one launch (start us, length us, event | category | flops | bytes accessed | tf_op | source)
XLA Modules:
  0.0 138.1 jit_solution(16341221829617317882)
XLA Ops:
  0.6 0.8 copy.32
  1.4 0.7 reduce_max.9
  2.1 0.1 squeeze.13
  2.2 0.2 fusion.1
  2.4 0.1 div.36
  2.5 0.1 div.37
  2.6 0.1 sub.51
  2.7 0.1 sub.52
  2.8 0.8 copy.31
  3.6 0.7 reshape.163.ids_ref
  4.3 1.9 %multiply_convert_fusion.c_ref = bf16[1024,128]{1,0:T(8,128)(2,1)} fusion(f32[1024]{0:T(1024)S(1)} %exponential_divide_fusion, bf16[1,128,8,128]{3,2,1,0:T(8,128)(2,1)} %param.13), kind=kLoop, calls=%fused_computation | loop fusion | flops 393216 | bytes 528384 | tf_op jit(solution)/shard_map/convert_element_type | solution.py:166
  6.1 5.2 %pack.1 = (bf16[16,528,128]{2,1,0:T(8,128)(2,1)}, s32[1,1024]{1,0:T(1,128)}) custom-call(s32[1,1024]{1,0:T(1,128)} %reshape.163.ids_ref, bf16[1024,128]{1,0:T(8,128)(2,1)} %bitcast.19, bf16[1024,128]{1,0:T(8,128)(2,1)} %bitcast.20, bf16[1024,128]{1,0:T(8,128)(2,1)} %bitcast.21, bf16[1024,128]{1,0:T(8,128)(2,1)} %multiply_convert_fusion.c_ref), custom_call_target="tpu_custom_call" | custom-call | tf_op jit(solution)/shard_map/pack/pallas_call | solution.py:171
  11.3 55.4 %all_to_all.10.recv_ref = bf16[16,528,128]{2,1,0:T(8,128)(2,1)} all-to-all(bf16[16,528,128]{2,1,0:T(8,128)(2,1)} %get-tuple-element.16), channel_id=1, replica_groups=mesh['dp'=2,'head'=16] {'head'}, dimensions={0} | all-to-all | bytes 4325376 | tf_op jit(solution)/shard_map/all_to_all | solution.py:183
  66.7 8.9 %attend.1 = (bf16[16,512,128]{2,1,0:T(8,128)(2,1)}, f32[4,8,128]{2,1,0:T(8,128)}) custom-call(f32[4]{0:T(128)} %sink_ref.1, bf16[16,528,128]{2,1,0:T(8,128)(2,1)} %all_to_all.10.recv_ref), custom_call_target="tpu_custom_call" | custom-call | tf_op jit(solution)/shard_map/attend/pallas_call | solution.py:186
  75.6 0.0 copy-start.2
  75.6 5.9 %all-to-all-start.1 = ((bf16[16,512,128]{2,1,0:T(8,128)(2,1)}), bf16[16,512,128]{2,1,0:T(8,128)(2,1)S(1)}, u32[]{:S(2)}, u32[]{:S(2)}) async-start(bf16[16,512,128]{2,1,0:T(8,128)(2,1)} %get-tuple-element.17), calls=%async_computation.1 | async-start | bytes 4194304 | tf_op jit(solution)/shard_map/all_to_all | solution.py:198
  81.5 0.2 div.44
  81.7 0.1 sub.55
  81.8 0.1 squeeze.16
  81.9 0.0 copy-done.2
  81.9 1.0 copy.37.target_ref
  83.0 0.2 copy.35
  83.2 0.9 div.40.gate_ref
  84.1 0.0 copy-start.1
  84.1 0.8 slice_reduce_fusion
  85.0 1.3 collective-permute-start
  86.2 1.5 %collective-permute-done = f32[4]{0:T(128)S(1)} collective-permute-done((f32[4]{0:T(128)S(1)}, f32[4]{0:T(128)S(1)}, u32[]{:S(2)}, u32[]{:S(2)}) %collective-permute-start) | collective-permute-done | bytes 48 | tf_op jit(solution)/shard_map/ppermute | solution.py:203
  87.7 0.5 add.3
  88.2 40.7 %all-to-all-done.1.back_ref = bf16[16,512,128]{2,1,0:T(8,128)(2,1)S(1)} async-done(((bf16[16,512,128]{2,1,0:T(8,128)(2,1)}), bf16[16,512,128]{2,1,0:T(8,128)(2,1)S(1)}, u32[]{:S(2)}, u32[]{:S(2)}) %all-to-all-start.1) | async-done | bytes 2097184 | tf_op jit(solution)/shard_map/all_to_all | solution.py:198
  129.0 0.0 copy-start
  129.0 1.3 copy-done
  130.3 5.5 %unpack.1 = (bf16[1024,128]{1,0:T(8,128)(2,1)}, bf16[1024,128]{1,0:T(8,128)(2,1)}, bf16[1024,128]{1,0:T(8,128)(2,1)}, bf16[1024,128]{1,0:T(8,128)(2,1)}, f32[1024,1]{1,0:T(8,128)}) custom-call(s32[1024,1]{1,0:T(8,128)} %copy.37.target_ref, f32[1024,1]{1,0:T(8,128)} %div.40.gate_ref, bf16[1024,128]{1,0:T(8,128)(2,1)} %bitcast.18, bf16[16,512,128]{2,1,0:T(8,128)(2,1)} %copy-done), custom_call_target="tpu_custom_call" | custom-call | tf_op jit(solution)/shard_map/unpack/pallas_call | solution.py:207
  135.8 1.2 reduce.1
  137.0 0.1 reshape.173
  137.1 0.1 reshape.172
  137.2 0.2 multiply_reduce_fusion
  137.4 0.1 copy.38
  137.5 0.0 copy-done.1
  137.5 0.6 subtract_multiply_fusion
  (2 shorter events, 0.0 us)
Async XLA Ops:
  75.6 6.3 %copy-start.2 = (s32[1,1024]{1,0:T(1,128)S(1)}, s32[1,1024]{1,0:T(1,128)}, u32[]{:S(2)}) copy-start(s32[1,1024]{1,0:T(1,128)} %get-tuple-element.15) | copy-start | bytes 12292
  75.6 53.4 %all-to-all-start.1 = ((bf16[16,512,128]{2,1,0:T(8,128)(2,1)}), bf16[16,512,128]{2,1,0:T(8,128)(2,1)S(1)}, u32[]{:S(2)}, u32[]{:S(2)}) async-start(bf16[16,512,128]{2,1,0:T(8,128)(2,1)} %get-tuple-element.17), calls=%async_computation.1 | async-start | bytes 4194304 | tf_op jit(solution)/shard_map/all_to_all | solution.py:198
  84.1 53.4 %copy-start.1 = (f32[1,128,8]{1,2,0:T(8,128)S(1)}, f32[1,128,8]{1,2,0:T(8,128)}, u32[]{:S(2)}) copy-start(f32[1,128,8]{1,2,0:T(8,128)} %param.11) | copy-start | bytes 12292
  85.0 2.8 %collective-permute-start = (f32[4]{0:T(128)S(1)}, f32[4]{0:T(128)S(1)}, u32[]{:S(2)}, u32[]{:S(2)}) collective-permute-start(f32[4]{0:T(128)S(1)} %slice_reduce_fusion), channel_id=1, source_target_pairs={{0,16},{16,0},{1,17},{17,1},{2,18},{18,2},{3,19},{19,3},{4,20},{20... | collective-permute-start | bytes 56 | tf_op jit(solution)/shard_map/ppermute | solution.py:203
  129.0 1.4 copy-start
